TPU v7x, 32 devices: a whole 2x2x4 slice. The times are simulated.
32 devices in a mesh: trial: 16 (over z, y, x), factor: 2 (over core).
Axes of the slice: x: 2, y: 2, z: 4, core: 2. Of those that a mesh axis runs over, the one named last changes fastest.
Arguments:
- observed: float32 [64, 32, 128], P('trial'), may hold values from -6 to 6
- trial_mean: float32 [64], P('trial'), may hold values from -4 to 4
- correlations: float32 [64, 2], P('trial'), may hold values from 0.1 to 0.7
- noise_var: float32 [64], P('trial'), may hold values from 2 to 8
- plot_slot: int32 [64, 32, 128], P('trial'), may hold values from 0 to 2047
- row_count: int32 [64], P('trial'), may hold values from 8 to 32, as said below
- col_count: int32 [64], P('trial'), may hold values from 64 to 128, as said below
- panel_list: int32 [64, 16], P('trial'), may hold values from 0 to 191, as said below
- scores: bfloat16 [128, 24576], P('factor', 'trial'), may hold values from -0.5 to 0.5
- loadings: float32 [64, 128], P('trial', 'factor'), may hold values from -5 to 5
- score_precision: float32 [128], P('factor'), may hold values from 20 to 80
Outputs:
- score_gradient: float32 [128, 24576], P('factor', 'trial')
- loading_gradient: float32 [64, 128], P('trial', 'factor')
Inputs may be any that keep to these rules, and one draw needn't show every extreme that they name: `panel_list`: panel p is owned by index p // 12 of trial. Among the 64 entries of each aligned block of 4 trials, no owner holds more than 8 of them, and in every block some owner holds exactly that many. Entries may repeat. `row_count`: the first trial uses all 32 rows. `col_count`: the first trial uses all 128 columns.
All inputs are finite; a program needn't handle non-finite values.
Results may differ from a plain program's by a relative error of at most 0.0023.
Values may be sent and summed in bfloat16 or wider, within the bound.
A program may use at most 64 MiB of HBM per device.

v0:
```python
import jax
import jax.numpy as jnp
from jax import lax
from jax.sharding import PartitionSpec as P

PANEL = 128
score_step = 0.005
load_step = 0.02


def sweep_axis(values_in, corr_value, position, limit_count, axis_number):
    factor_scale = 1.0 / (1.0 - corr_value * corr_value)
    interior = ((position > 0) & (position < limit_count - 1)).astype(values_in.dtype)
    padding = [(0, 0)] * values_in.ndim
    padding[axis_number] = (1, 1)
    padded = jnp.pad(values_in, padding)
    length = values_in.shape[axis_number]
    lower_side = lax.slice_in_dim(padded, 0, length, axis=axis_number)
    upper_side = lax.slice_in_dim(padded, 2, length + 2, axis=axis_number)
    result = factor_scale * (
        (1.0 + corr_value * corr_value * interior) * values_in
        - corr_value * (lower_side + upper_side)
    )
    return jnp.where(position < limit_count, result, 0.0)


def body(
    observed,
    trial_mean,
    correlations,
    noise_var,
    plot_slot,
    row_count,
    col_count,
    panel_list,
    scores,
    loadings,
    score_precision,
):
    trial_count = lax.axis_size("trial")
    per_dev = panel_list.shape[0]
    per_trial = panel_list.shape[1]
    required_count = per_dev * per_trial
    most_count = 2 * required_count // trial_count
    slots_total = trial_count * most_count
    latent_factor_count = scores.shape[0]
    owned_panels = scores.shape[1] // PANEL
    slots_trial = per_trial * PANEL
    wanted = panel_list.reshape(required_count)
    owner_of = wanted // owned_panels
    local_of = wanted - owner_of * owned_panels
    later_pos = lax.broadcasted_iota(jnp.int32, (required_count, required_count), 0)
    other_pos = lax.broadcasted_iota(jnp.int32, (required_count, required_count), 1)
    earlier = (owner_of[None, :] == owner_of[:, None]) & (other_pos < later_pos)
    rank_of = jnp.sum(earlier.astype(jnp.int32), axis=1)
    position = owner_of * most_count + rank_of
    placer_int = (
        position[None, :] == lax.broadcasted_iota(jnp.int32, (slots_total, required_count), 0)
    ).astype(jnp.int32)
    request = jnp.sum(placer_int * (local_of[None, :] + 1), axis=1) - 1
    placer = placer_int.astype(jnp.float32)
    incoming = lax.all_to_all(request, "trial", split_axis=0, concat_axis=0, tiled=True)
    picker = (
        incoming[None, :] == lax.broadcasted_iota(jnp.int32, (owned_panels, slots_total), 0)
    ).astype(jnp.float32)
    grid_shape = observed.shape
    plot_count = grid_shape[1] * grid_shape[2]
    row_index = lax.broadcasted_iota(jnp.int32, grid_shape, 1)
    col_index = lax.broadcasted_iota(jnp.int32, grid_shape, 2)
    row_upper_limit = row_count[:, None, None]
    col_limit = col_count[:, None, None]
    active = (row_index < row_upper_limit) & (col_index < col_limit)
    flat_slot = plot_slot.reshape(per_dev, plot_count)
    panel_of_plot = flat_slot // PANEL
    cell_of_plot = flat_slot - panel_of_plot * PANEL
    panel_onehot_matrix = (
        panel_of_plot[:, :, None]
        == lax.broadcasted_iota(jnp.int32, (per_dev, plot_count, per_trial), 2)
    ).astype(jnp.float32)
    cell_match = cell_of_plot[:, :, None] == lax.broadcasted_iota(
        jnp.int32, (per_dev, plot_count, PANEL), 2
    )
    correlation_row_values = correlations[:, 0][:, None, None]
    corr_cols = correlations[:, 1][:, None, None]

    def fetch(current):
        whole = lax.all_gather(current, "trial", axis=1, tiled=True)
        grouped = whole.reshape(latent_factor_count, -1, PANEL)
        panel_total = grouped.shape[1]
        chooser = (
            wanted[None, :] == lax.broadcasted_iota(jnp.int32, (panel_total, required_count), 0)
        ).astype(jnp.bfloat16)
        picked = jnp.einsum(
            "kqc,qn->knc", grouped, chooser, preferred_element_type=jnp.float32
        ).astype(jnp.bfloat16)
        return picked.reshape(latent_factor_count, per_dev, slots_trial)

    def evaluate(current, loads_now):
        table = fetch(current)
        table_wide = table.astype(jnp.float32)
        partial_effect = jnp.einsum(
            "ktn,tk->tn", table_wide, loads_now, precision=lax.Precision.HIGHEST
        )
        effect = lax.psum(partial_effect, "factor")
        effect_table_grid = effect.reshape(per_dev, per_trial, PANEL)
        rows_picked = jnp.einsum(
            "jwo,jom->jwm", panel_onehot_matrix, effect_table_grid, precision=lax.Precision.HIGHEST
        )
        fitted = jnp.sum(jnp.where(cell_match, rows_picked, 0.0), axis=2).reshape(grid_shape)
        residual = jnp.where(active, observed - trial_mean[:, None, None] - fitted, 0.0)
        across = sweep_axis(residual, corr_cols, col_index, col_limit, 2)
        weighted = (
            sweep_axis(across, correlation_row_values, row_index, row_upper_limit, 1)
            / noise_var[:, None, None]
        )
        dispersion_amount = jnp.where(
            cell_match, weighted.reshape(per_dev, plot_count)[:, :, None], 0.0
        )
        slot_weight = jnp.einsum(
            "boy,bom->bym", panel_onehot_matrix, dispersion_amount, precision=lax.Precision.HIGHEST
        ).reshape(per_dev, slots_trial)
        load_grad = -jnp.einsum(
            "ktn,tn->tk", table_wide, slot_weight, precision=lax.Precision.HIGHEST
        )
        returned = -(loads_now.T[:, :, None] * slot_weight[None, :, :])
        returned = returned.reshape(latent_factor_count, required_count, PANEL)
        outgoing = jnp.einsum("jn,knc->kjc", placer, returned, precision=lax.Precision.HIGHEST)
        arrived = lax.all_to_all(outgoing, "trial", split_axis=1, concat_axis=1, tiled=True)
        summed = jnp.einsum("qj,kjc->kqc", picker, arrived, precision=lax.Precision.HIGHEST)
        score_grad = score_precision[:, None] * current.astype(jnp.float32) + summed.reshape(
            latent_factor_count, owned_panels * PANEL
        )
        return (score_grad, load_grad)

    first_scores, first_loads = evaluate(scores, loadings)
    new_scores = (scores.astype(jnp.float32) - score_step * first_scores).astype(jnp.bfloat16)
    new_loads = loadings - load_step * first_loads
    return evaluate(new_scores, new_loads)


def solution(mesh):
    in_specs = (
        P("trial", None, None),
        P("trial"),
        P("trial", None),
        P("trial"),
        P("trial", None, None),
        P("trial"),
        P("trial"),
        P("trial", None),
        P("factor", "trial"),
        P("trial", "factor"),
        P("factor"),
    )
    out_specs = (P("factor", "trial"), P("trial", "factor"))
    return jax.shard_map(body, mesh=mesh, in_specs=in_specs, out_specs=out_specs, check_vma=False)
```

profile of v0, /device:TPU:14, one launch (start us, length us, event | category | flops | bytes accessed | tf_op | source)
XLA Modules:
  0.0 437.1 jit_solution(3423635285913149859)
XLA Ops:
  7.9 0.8 eq.65
  9.7 7.1 %all-to-all-start.1 = ((s32[16,8,1]{1,2,0:T(1,128)}), s32[16,8,1]{1,2,0:T(1,128)S(1)}, u32[]{:S(2)}, u32[]{:S(2)}) async-start(s32[16,8,1]{1,2,0:T(1,128)} %bitcast.12), calls=%async_computation.1 | async-start | bytes 16384 | tf_op jit(solution)/shard_map/all_to_all | solution.py:62
  18.9 0.8 slice_bitcast_fusion.1
  19.7 0.8 subtract_divide_fusion.1
  20.4 0.9 bitcast_subtract_fusion.2
  21.4 57.7 %all-gather.3.cloned.1.call-done = bf16[64,24576]{1,0:T(8,128)(2,1)} async-done(((bf16[64,1536]{1,0:T(8,128)(2,1)}), bf16[64,24576]{1,0:T(8,128)(2,1)}) %all-gather.3.cloned.1.call-update) | async-done | bytes 3145744 | tf_op jit(solution)/shard_map/all_gather | solution.py:87
  79.1 2.7 copy.52
  82.8 1.5 fusion.30
  84.4 3.7 psum.14
  88.2 4.5 %select_reduce_fusion.1 = f32[4,4096]{1,0:T(4,128)S(1)} fusion(f32[4,16,128]{2,1,0:T(8,128)S(1)} %psum.14, s32[4,4096]{1,0:T(4,128)S(1)} %get-tuple-element.4, s32[4,4096]{1,0:T(4,128)S(1)} %get-tuple-element.5), kind=kOutput, calls=%fused_computation.5 | convolution fusion | flops 409190400 | bytes 229376 | tf_op jit(solution)/shard_map/jwo,jom->jwm/dot_general | solution.py:106
  93.1 4.7 %fusion.2 = f32[4,16,128]{2,1,0:T(8,128)S(1)} fusion(f32[4,4096]{1,0:T(4,128)S(1)} %bitcast.142, s32[4,4096]{1,0:T(4,128)S(1)} %get-tuple-element.4, s32[4,4096]{1,0:T(4,128)S(1)} %get-tuple-element.5), kind=kOutput, calls=%fused_computation.3 | convolution fusion | flops 407109632 | bytes 229376 | tf_op jit(solution)/shard_map/boy,bom->bym/dot_general | solution.py:119
  97.8 8.8 %convolution_bitcast_fusion.1 = f32[64,128,128]{1,2,0:T(8,128)} fusion(f32[64,128]{1,0:T(8,128)S(1)} %bitcast.143, f32[64,64]{1,0:T(8,128)S(1)} %copy.30, s32[64]{0:T(128)S(1)} %multiply_add_fusion), kind=kOutput, calls=%fused_computation.18 | convolution fusion | flops 806379520 | bytes 4243712 | tf_op jit(solution)/shard_map/jn,knc->kjc/dot_general | solution.py:127
  106.6 5.4 %copy.32 = f32[64,128,128]{2,0,1:T(8,128)} copy(f32[64,128,128]{1,2,0:T(8,128)} %convolution_bitcast_fusion.1) | data formatting | bytes 8388608 | tf_op jit(solution)/shard_map/jn,knc->kjc/transpose | solution.py:127
  112.1 5.7 %all-to-all-start = ((f32[64,128,128]{2,0,1:T(8,128)}), f32[64,128,128]{2,0,1:T(8,128)}, u32[]{:S(2)}, u32[]{:S(2)}) async-start(f32[64,128,128]{2,0,1:T(8,128)} %copy.32), calls=%async_computation | async-start | bytes 8388608 | tf_op jit(solution)/shard_map/all_to_all | solution.py:128
  119.7 94.7 %all-to-all-done = f32[64,128,128]{2,0,1:T(8,128)} async-done(((f32[64,128,128]{2,0,1:T(8,128)}), f32[64,128,128]{2,0,1:T(8,128)}, u32[]{:S(2)}, u32[]{:S(2)}) %all-to-all-start) | async-done | bytes 4194336 | tf_op jit(solution)/shard_map/all_to_all | solution.py:128
  214.4 5.8 %fusion.6 = f32[64,128,12]{1,2,0:T(8,128)S(1)} fusion(f32[64,128,128]{2,0,1:T(8,128)} %all-to-all-done, s32[128]{0:T(128)S(1)} %eq.73), kind=kOutput, calls=%fused_computation.9 | convolution fusion | flops 150996480 | bytes 4588032 | tf_op jit(solution)/shard_map/qj,kjc->kqc/dot_general | solution.py:129
  220.2 0.9 fusion.38
  221.1 1.3 fusion.28
  222.5 65.6 %all-gather.5.cloned.1.call-done = bf16[64,24576]{1,0:T(8,128)(2,1)} async-done(((bf16[64,1536]{1,0:T(8,128)(2,1)}), bf16[64,24576]{1,0:T(8,128)(2,1)}) %all-gather.5.cloned.1.call-update) | async-done | bytes 3145744 | tf_op jit(solution)/shard_map/all_gather | solution.py:87
  288.1 2.7 copy.57
  290.9 0.7 fusion.19
  291.9 1.5 fusion.26
  293.5 3.6 psum.15
  297.1 4.5 %select_reduce_fusion = f32[4,4096]{1,0:T(4,128)S(1)} fusion(f32[4,16,128]{2,1,0:T(8,128)S(1)} %psum.15, s32[4,4096]{1,0:T(4,128)S(1)} %get-tuple-element.4, s32[4,4096]{1,0:T(4,128)S(1)} %get-tuple-element.5), kind=kOutput, calls=%fused_computation.2 | convolution fusion | flops 409190400 | bytes 229376 | tf_op jit(solution)/shard_map/jwo,jom->jwm/dot_general | solution.py:106
  301.9 4.7 %fusion = f32[4,16,128]{2,1,0:T(8,128)S(1)} fusion(f32[4,4096]{1,0:T(4,128)S(1)} %bitcast.141, s32[4,4096]{1,0:T(4,128)S(1)} %get-tuple-element.4, s32[4,4096]{1,0:T(4,128)S(1)} %get-tuple-element.5), kind=kOutput, calls=%fused_computation | convolution fusion | flops 407109632 | bytes 229376 | tf_op jit(solution)/shard_map/boy,bom->bym/dot_general | solution.py:119
  306.7 8.8 %convolution_bitcast_fusion = f32[64,128,128]{1,2,0:T(8,128)} fusion(f32[64,128]{1,0:T(8,128)S(1)} %bitcast.145, f32[64,64]{1,0:T(8,128)S(1)} %copy.35, s32[64]{0:T(128)S(1)} %multiply_add_fusion), kind=kOutput, calls=%fused_computation.17 | convolution fusion | flops 806379520 | bytes 4243712 | tf_op jit(solution)/shard_map/jn,knc->kjc/dot_general | solution.py:127
  315.5 5.4 %copy.37 = f32[64,128,128]{2,0,1:T(8,128)} copy(f32[64,128,128]{1,2,0:T(8,128)} %convolution_bitcast_fusion) | data formatting | bytes 8388608 | tf_op jit(solution)/shard_map/jn,knc->kjc/transpose | solution.py:127
  320.9 6.1 %all-to-all-start.2 = ((f32[64,128,128]{2,0,1:T(8,128)}), f32[64,128,128]{2,0,1:T(8,128)}, u32[]{:S(2)}, u32[]{:S(2)}) async-start(f32[64,128,128]{2,0,1:T(8,128)} %copy.37), calls=%async_computation.2 | async-start | bytes 8388608 | tf_op jit(solution)/shard_map/all_to_all | solution.py:128
  327.0 1.3 fusion.24
  328.9 94.4 %all-to-all-done.2 = f32[64,128,128]{2,0,1:T(8,128)} async-done(((f32[64,128,128]{2,0,1:T(8,128)}), f32[64,128,128]{2,0,1:T(8,128)}, u32[]{:S(2)}, u32[]{:S(2)}) %all-to-all-start.2) | async-done | bytes 4194336 | tf_op jit(solution)/shard_map/all_to_all | solution.py:128
  423.3 5.8 %fusion.4 = f32[64,128,12]{1,2,0:T(8,128)S(1)} fusion(f32[64,128,128]{2,0,1:T(8,128)} %all-to-all-done.2, s32[128]{0:T(128)S(1)} %eq.73), kind=kOutput, calls=%fused_computation.7 | convolution fusion | flops 150996480 | bytes 4588032 | tf_op jit(solution)/shard_map/qj,kjc->kqc/dot_general | solution.py:129
  429.1 0.9 bitcast_add_fusion
  (57 shorter events, 8.5 us)
Async XLA Ops:
  7.2 71.9 %all-gather.3.cloned.1.call-start = ((), (), s32[]{:S(2)}) async-start(), calls=%async_computation.3 | async-start | bytes 3342336 | tf_op jit(solution)/shard_map/all_gather | solution.py:87
  9.7 102.4 %all-to-all-start.1 = ((s32[16,8,1]{1,2,0:T(1,128)}), s32[16,8,1]{1,2,0:T(1,128)S(1)}, u32[]{:S(2)}, u32[]{:S(2)}) async-start(s32[16,8,1]{1,2,0:T(1,128)} %bitcast.12), calls=%async_computation.1 | async-start | bytes 16384 | tf_op jit(solution)/shard_map/all_to_all | solution.py:62
  81.8 1.0 copy-start.5
  88.1 4.5 %copy-start.2 = (f32[4,32,128]{2,1,0:T(8,128)S(1)}, f32[4,32,128]{2,1,0:T(8,128)}, u32[]{:S(2)}) copy-start(f32[4,32,128]{2,1,0:T(8,128)} %param.11) | copy-start | bytes 196612
  88.1 4.5 %copy-start.3 = (s32[4]{0:T(128)S(1)}, s32[4]{0:T(128)}, u32[]{:S(2)}) copy-start(s32[4]{0:T(128)} %param.17) | copy-start | bytes 52
  88.1 4.5 %copy-start.4 = (s32[4]{0:T(128)S(1)}, s32[4]{0:T(128)}, u32[]{:S(2)}) copy-start(s32[4]{0:T(128)} %param.16) | copy-start | bytes 52
  88.2 4.5 %copy-start.6 = (f32[4]{0:T(128)S(1)}, f32[4]{0:T(128)}, u32[]{:S(2)}) copy-start(f32[4]{0:T(128)} %param.12) | copy-start | bytes 52
  88.2 4.7 %copy-start.7 = (f32[4]{0:T(128)S(1)}, f32[4]{0:T(128)}, u32[]{:S(2)}) copy-start(f32[4]{0:T(128)} %param.14) | copy-start | bytes 52
  112.1 102.3 %all-to-all-start = ((f32[64,128,128]{2,0,1:T(8,128)}), f32[64,128,128]{2,0,1:T(8,128)}, u32[]{:S(2)}, u32[]{:S(2)}) async-start(f32[64,128,128]{2,0,1:T(8,128)} %copy.32), calls=%async_computation | async-start | bytes 8388608 | tf_op jit(solution)/shard_map/all_to_all | solution.py:128
  117.8 102.4 %copy-start.1 = (bf16[64,1536]{1,0:T(8,128)(2,1)S(1)}, bf16[64,1536]{1,0:T(8,128)(2,1)}, u32[]{:S(2)}) copy-start(bf16[64,1536]{1,0:T(8,128)(2,1)} %param.19) | copy-start | bytes 589828
  117.8 102.4 %copy-start.8 = (f32[64]{0:T(128)S(1)}, f32[64]{0:T(128)}, u32[]{:S(2)}) copy-start(f32[64]{0:T(128)} %param.21) | copy-start | bytes 772
  117.8 170.3 %all-gather.5.cloned.1.call-start = ((), (), s32[]{:S(2)}) async-start(), calls=%async_computation.4 | async-start | bytes 3342336 | tf_op jit(solution)/shard_map/all_gather | solution.py:87
  320.9 102.4 %all-to-all-start.2 = ((f32[64,128,128]{2,0,1:T(8,128)}), f32[64,128,128]{2,0,1:T(8,128)}, u32[]{:S(2)}, u32[]{:S(2)}) async-start(f32[64,128,128]{2,0,1:T(8,128)} %copy.37), calls=%async_computation.2 | async-start | bytes 8388608 | tf_op jit(solution)/shard_map/all_to_all | solution.py:128
  327.0 102.1 %copy-start = (bf16[64,1536]{1,0:T(8,128)(2,1)S(1)}, bf16[64,1536]{1,0:T(8,128)(2,1)}, u32[]{:S(2)}) copy-start(bf16[64,1536]{1,0:T(8,128)(2,1)} %fusion.38) | copy-start | bytes 589828
Sparse Core Ops, SparseCore 0:
  10.7 68.3 all-gather.2
  221.3 66.8 all-gather.4
where the time goes:
time: 441 us; the launch traced here: 437 us
  waiting for transfers between devices  313 us (71%)
  matrix products  54.7 us (12%)
  local copies, waits for them, and re-layouts  20.7 us (5%)
  starting transfers between devices  19.6 us (4%)
  between operations  14.6 us (3%)
  blocking collectives  7.28 us (2%)
  other arithmetic  7.07 us (2%)
    all_to_all x2, waiting for transfers between devices, evaluate(): lax.all_to_all(outgoing, 'trial', split_axis=1, concat_axis=1, tiled=True)  189 us
    all_gather x2, waiting for transfers between devices, fetch(): whole = lax.all_gather(current, 'trial', axis=1, tiled=True)  123 us
    dot_general x2, matrix products, evaluate(): jnp.einsum('jn,knc->kjc', placer, returned, precision=lax.Precision.HIGHEST)  17.7 us
    all_to_all x2, starting transfers between devices, evaluate(): lax.all_to_all(outgoing, 'trial', split_axis=1, concat_axis=1, tiled=True)  11.8 us
    dot_general x2, matrix products, evaluate(): jnp.einsum('qj,kjc->kqc', picker, arrived, precision=lax.Precision.HIGHEST)  11.6 us
    transpose x2, local copies, waits for them, and re-layouts, evaluate(): jnp.einsum('jn,knc->kjc', placer, returned, precision=lax.Precision.HIGHEST)  10.8 us
    dot_general x2, matrix products, evaluate(): jnp.einsum('boy,bom->bym', panel_onehot_matrix, dispersion_amount, precis...  9.44 us
    dot_general x2, matrix products, evaluate(): jnp.einsum('jwo,jom->jwm', panel_onehot_matrix, effect_table_grid, precis...  8.93 us
  transfers between devices with their start and end apart: 5, of which 4 were waited for; matrix products, arithmetic and copies ran while one was open for 9% of the time, Pallas kernels for 0%

commit v1 on v0

--- a/solution.py
+++ b/solution.py
@@ -84,7 +84,16 @@
     corr_cols = correlations[:, 1][:, None, None]
 
     def fetch(current):
-        whole = lax.all_gather(current, "trial", axis=1, tiled=True)
+        ways = lax.axis_size("trial")
+        up = [(d, (d + 1) % ways) for d in range(ways)]
+        down = [(d, (d - 1) % ways) for d in range(ways)]
+        earlier_2, later = ([current], [current])
+        for _ in range(ways // 2):
+            earlier_2.append(lax.ppermute(earlier_2[-1], "trial", up))
+        for _ in range((ways - 1) // 2):
+            later.append(lax.ppermute(later[-1], "trial", down))
+        line = jnp.concatenate([*earlier_2[::-1], *later[1:]], axis=1)
+        whole = jnp.roll(line, (lax.axis_index("trial") - ways // 2) * current.shape[1], axis=1)
         grouped = whole.reshape(latent_factor_count, -1, PANEL)
         panel_total = grouped.shape[1]
         chooser = (

time: 441 us -> 455 us (1.032)
  starting transfers between devices: 19.6 us -> 84.7 us
  waiting for transfers between devices: 313 us -> 269 us
  between operations: 14.6 us -> 1.93 us
    all_gather x2 -> x0, waiting for transfers between devices: 123 us -> none  [fetch(): whole = lax.all_gather(current, 'trial', axis=1, tiled=True)]
    ppermute x0 -> x30, waiting for transfers between devices: none -> 81.2 us  [the longest x16 40.9 us: fetch(): earlier_2.append(lax.ppermute(earlier_2[-1], 'trial', up))]
    ppermute x0 -> x30, starting transfers between devices: none -> 52 us  [the longest x14 27.6 us: fetch(): later.append(lax.ppermute(later[-1], 'trial', down))]
    all_to_all x2, starting transfers between devices: 11.8 us -> 27.2 us  [evaluate(): lax.all_to_all(outgoing, 'trial', split_axis=1, concat_axis=1, tiled=True)]
    unnamed x2 -> x4, other arithmetic: 0.21 us -> 4.99 us
  transfers between devices with their start and end apart: 5 -> 33, of which waited for: 4 -> 25; matrix products, arithmetic and copies ran while one was open for 9% -> 9% of each run, Pallas kernels for 0% -> 0%
where the time goes in v1:
time: 455 us; the launch traced here: 448 us
  waiting for transfers between devices  269 us (59%)
  starting transfers between devices  84.7 us (19%)
  matrix products  54.8 us (12%)
  local copies, waits for them, and re-layouts  19 us (4%)
  other arithmetic  11.1 us (2%)
  blocking collectives  7.39 us (2%)
    all_to_all x2, waiting for transfers between devices, evaluate(): lax.all_to_all(outgoing, 'trial', split_axis=1, concat_axis=1, tiled=True)  188 us
    ppermute x16, waiting for transfers between devices, fetch(): earlier_2.append(lax.ppermute(earlier_2[-1], 'trial', up))  40.9 us
    ppermute x14, waiting for transfers between devices, fetch(): later.append(lax.ppermute(later[-1], 'trial', down))  40.3 us
    ppermute x14, starting transfers between devices, fetch(): later.append(lax.ppermute(later[-1], 'trial', down))  27.6 us
    all_to_all x2, starting transfers between devices, evaluate(): lax.all_to_all(outgoing, 'trial', split_axis=1, concat_axis=1, tiled=True)  27.2 us
    ppermute x16, starting transfers between devices, fetch(): earlier_2.append(lax.ppermute(earlier_2[-1], 'trial', up))  24.5 us
    dot_general x2, matrix products, evaluate(): jnp.einsum('jn,knc->kjc', placer, returned, precision=lax.Precision.HIGHEST)  17.7 us
    dot_general x2, matrix products, evaluate(): jnp.einsum('qj,kjc->kqc', picker, arrived, precision=lax.Precision.HIGHEST)  11.6 us
  transfers between devices with their start and end apart: 33, of which 25 were waited for; matrix products, arithmetic and copies ran while one was open for 9% of the time, Pallas kernels for 0%

profile of v1, /device:TPU:14, one launch (start us, length us, event | category | flops | bytes accessed | tf_op | source)
XLA Modules:
  0.0 448.0 jit_solution(11430789534005772794)
XLA Ops:
  3.8 4.9 %collective-permute-done = bf16[64,1536]{1,0:T(8,128)(2,1)S(1)} collective-permute-done((bf16[64,1536]{1,0:T(8,128)(2,1)}, bf16[64,1536]{1,0:T(8,128)(2,1)S(1)}, u32[]{:S(2)}, u32[]{:S(2)}) %collective-permute-start) | collective-permute-done | bytes 196640 | tf_op jit(solution)/shard_map/ppermute | solution.py:92
  8.7 4.7 %collective-permute-start.1 = (bf16[64,1536]{1,0:T(8,128)(2,1)S(1)}, bf16[64,1536]{1,0:T(8,128)(2,1)S(1)}, u32[]{:S(2)}, u32[]{:S(2)}) collective-permute-start(bf16[64,1536]{1,0:T(8,128)(2,1)S(1)} %collective-permute-done), channel_id=1, source_target_pairs={{0,2},{2,4},{4,6},{6,8},{8,10},{10,12},{12,14},{14,16},{16,18},{18... | collective-permute-start | bytes 589832 | tf_op jit(solution)/shard_map/ppermute | solution.py:92
  14.0 5.5 %all-to-all-start.1 = ((s32[16,8,1]{1,2,0:T(1,128)}), s32[16,8,1]{1,2,0:T(1,128)S(1)}, u32[]{:S(2)}, u32[]{:S(2)}) async-start(s32[16,8,1]{1,2,0:T(1,128)} %bitcast.12), calls=%async_computation.1 | async-start | bytes 16384 | tf_op jit(solution)/shard_map/all_to_all | solution.py:62
  23.4 3.7 collective-permute-done.2
  28.6 3.5 collective-permute-done.9
  36.9 4.5 %collective-permute-done.10 = bf16[64,1536]{1,0:T(8,128)(2,1)S(1)} collective-permute-done((bf16[64,1536]{1,0:T(8,128)(2,1)S(1)}, bf16[64,1536]{1,0:T(8,128)(2,1)S(1)}, u32[]{:S(2)}, u32[]{:S(2)}) %collective-permute-start.10) | collective-permute-done | bytes 196640 | tf_op jit(solution)/shard_map/ppermute | solution.py:94
  46.1 5.6 %collective-permute-done.11 = bf16[64,1536]{1,0:T(8,128)(2,1)S(1)} collective-permute-done((bf16[64,1536]{1,0:T(8,128)(2,1)S(1)}, bf16[64,1536]{1,0:T(8,128)(2,1)S(1)}, u32[]{:S(2)}, u32[]{:S(2)}) %collective-permute-start.11) | collective-permute-done | bytes 196640 | tf_op jit(solution)/shard_map/ppermute | solution.py:94
  57.8 5.7 %collective-permute-done.12 = bf16[64,1536]{1,0:T(8,128)(2,1)S(1)} collective-permute-done((bf16[64,1536]{1,0:T(8,128)(2,1)S(1)}, bf16[64,1536]{1,0:T(8,128)(2,1)S(1)}, u32[]{:S(2)}, u32[]{:S(2)}) %collective-permute-start.12) | collective-permute-done | bytes 196640 | tf_op jit(solution)/shard_map/ppermute | solution.py:94
  68.9 3.8 collective-permute-done.13
  75.4 4.7 %collective-permute-done.14 = bf16[64,1536]{1,0:T(8,128)(2,1)S(1)} collective-permute-done((bf16[64,1536]{1,0:T(8,128)(2,1)S(1)}, bf16[64,1536]{1,0:T(8,128)(2,1)S(1)}, u32[]{:S(2)}, u32[]{:S(2)}) %collective-permute-start.14) | collective-permute-done | bytes 196640 | tf_op jit(solution)/shard_map/ppermute | solution.py:94
  86.0 3.6 psum.14
  89.7 4.5 select_reduce_fusion.1
  94.7 4.7 %fusion.2 = f32[4,16,128]{2,1,0:T(8,128)S(1)} fusion(f32[4,4096]{1,0:T(4,128)S(1)} %bitcast.142, s32[4,4096]{1,0:T(4,128)S(1)} %get-tuple-element.5, s32[4,4096]{1,0:T(4,128)S(1)} %get-tuple-element.6), kind=kOutput, calls=%fused_computation.3 | convolution fusion | flops 407109632 | bytes 229376 | tf_op jit(solution)/shard_map/boy,bom->bym/dot_general | solution.py:128
  99.4 8.9 %convolution_bitcast_fusion.1 = f32[64,128,128]{1,2,0:T(8,128)} fusion(f32[64,128]{1,0:T(8,128)S(1)} %bitcast.143, f32[64,64]{1,0:T(8,128)S(1)} %copy.30, s32[64]{0:T(128)S(1)} %multiply_add_fusion), kind=kOutput, calls=%fused_computation.26 | convolution fusion | flops 806379520 | bytes 4243712 | tf_op jit(solution)/shard_map/jn,knc->kjc/dot_general | solution.py:136
  108.3 5.4 %copy.32 = f32[64,128,128]{2,0,1:T(8,128)} copy(f32[64,128,128]{1,2,0:T(8,128)} %convolution_bitcast_fusion.1) | data formatting | bytes 8388608 | tf_op jit(solution)/shard_map/jn,knc->kjc/transpose | solution.py:136
  113.7 13.0 %all-to-all-start = ((f32[64,128,128]{2,0,1:T(8,128)}), f32[64,128,128]{2,0,1:T(8,128)}, u32[]{:S(2)}, u32[]{:S(2)}) async-start(f32[64,128,128]{2,0,1:T(8,128)} %copy.32), calls=%async_computation | async-start | bytes 8388608 | tf_op jit(solution)/shard_map/all_to_all | solution.py:137
  128.0 94.3 %all-to-all-done = f32[64,128,128]{2,0,1:T(8,128)} async-done(((f32[64,128,128]{2,0,1:T(8,128)}), f32[64,128,128]{2,0,1:T(8,128)}, u32[]{:S(2)}, u32[]{:S(2)}) %all-to-all-start) | async-done | bytes 4194336 | tf_op jit(solution)/shard_map/all_to_all | solution.py:137
  222.3 5.8 %fusion.6 = f32[64,128,12]{1,2,0:T(8,128)S(1)} fusion(f32[64,128,128]{2,0,1:T(8,128)} %all-to-all-done, s32[128]{0:T(128)S(1)} %eq.75), kind=kOutput, calls=%fused_computation.13 | convolution fusion | flops 150996480 | bytes 4588032 | tf_op jit(solution)/shard_map/qj,kjc->kqc/dot_general | solution.py:138
  228.4 6.0 %collective-permute-done.15 = bf16[64,1536]{1,0:T(8,128)(2,1)S(1)} collective-permute-done((bf16[64,1536]{1,0:T(8,128)(2,1)S(1)}, bf16[64,1536]{1,0:T(8,128)(2,1)S(1)}, u32[]{:S(2)}, u32[]{:S(2)}) %collective-permute-start.15) | collective-permute-done | bytes 196640 | tf_op jit(solution)/shard_map/ppermute | solution.py:92
  236.5 5.8 %collective-permute-done.16 = bf16[64,1536]{1,0:T(8,128)(2,1)S(1)} collective-permute-done((bf16[64,1536]{1,0:T(8,128)(2,1)S(1)}, bf16[64,1536]{1,0:T(8,128)(2,1)S(1)}, u32[]{:S(2)}, u32[]{:S(2)}) %collective-permute-start.16) | collective-permute-done | bytes 196640 | tf_op jit(solution)/shard_map/ppermute | solution.py:92
  254.7 4.7 %collective-permute-done.18 = bf16[64,1536]{1,0:T(8,128)(2,1)S(1)} collective-permute-done((bf16[64,1536]{1,0:T(8,128)(2,1)S(1)}, bf16[64,1536]{1,0:T(8,128)(2,1)S(1)}, u32[]{:S(2)}, u32[]{:S(2)}) %collective-permute-start.18) | collective-permute-done | bytes 196640 | tf_op jit(solution)/shard_map/ppermute | solution.py:92
  262.7 4.7 %collective-permute-done.19 = bf16[64,1536]{1,0:T(8,128)(2,1)S(1)} collective-permute-done((bf16[64,1536]{1,0:T(8,128)(2,1)S(1)}, bf16[64,1536]{1,0:T(8,128)(2,1)S(1)}, u32[]{:S(2)}, u32[]{:S(2)}) %collective-permute-start.19) | collective-permute-done | bytes 196640 | tf_op jit(solution)/shard_map/ppermute | solution.py:92
  271.1 5.0 %collective-permute-done.20 = bf16[64,1536]{1,0:T(8,128)(2,1)S(1)} collective-permute-done((bf16[64,1536]{1,0:T(8,128)(2,1)S(1)}, bf16[64,1536]{1,0:T(8,128)(2,1)S(1)}, u32[]{:S(2)}, u32[]{:S(2)}) %collective-permute-start.20) | collective-permute-done | bytes 196640 | tf_op jit(solution)/shard_map/ppermute | solution.py:92
  293.7 3.9 collective-permute-done.29
  303.4 3.8 psum.15
  307.4 4.5 select_reduce_fusion
  312.4 4.7 %fusion = f32[4,16,128]{2,1,0:T(8,128)S(1)} fusion(f32[4,4096]{1,0:T(4,128)S(1)} %bitcast.141, s32[4,4096]{1,0:T(4,128)S(1)} %copy-done.4, s32[4,4096]{1,0:T(4,128)S(1)} %copy-done.6), kind=kOutput, calls=%fused_computation | convolution fusion | flops 407109632 | bytes 229376 | tf_op jit(solution)/shard_map/boy,bom->bym/dot_general | solution.py:128
  317.1 8.9 %convolution_bitcast_fusion = f32[64,128,128]{1,2,0:T(8,128)} fusion(f32[64,128]{1,0:T(8,128)S(1)} %bitcast.145, f32[64,64]{1,0:T(8,128)S(1)} %copy-done.2, s32[64]{0:T(128)S(1)} %copy-done.33), kind=kOutput, calls=%fused_computation.25 | convolution fusion | flops 806379520 | bytes 4243712 | tf_op jit(solution)/shard_map/jn,knc->kjc/dot_general | solution.py:136
  326.0 5.4 %copy.37 = f32[64,128,128]{2,0,1:T(8,128)} copy(f32[64,128,128]{1,2,0:T(8,128)} %convolution_bitcast_fusion) | data formatting | bytes 8388608 | tf_op jit(solution)/shard_map/jn,knc->kjc/transpose | solution.py:136
  331.4 14.1 %all-to-all-start.2 = ((f32[64,128,128]{2,0,1:T(8,128)}), f32[64,128,128]{2,0,1:T(8,128)}, u32[]{:S(2)}, u32[]{:S(2)}) async-start(f32[64,128,128]{2,0,1:T(8,128)} %copy.37), calls=%async_computation.2 | async-start | bytes 8388608 | tf_op jit(solution)/shard_map/all_to_all | solution.py:137
  347.4 93.7 %all-to-all-done.2 = f32[64,128,128]{2,0,1:T(8,128)} async-done(((f32[64,128,128]{2,0,1:T(8,128)}), f32[64,128,128]{2,0,1:T(8,128)}, u32[]{:S(2)}, u32[]{:S(2)}) %all-to-all-start.2) | async-done | bytes 4194336 | tf_op jit(solution)/shard_map/all_to_all | solution.py:137
  441.1 5.8 %fusion.4 = f32[64,128,12]{1,2,0:T(8,128)S(1)} fusion(f32[64,128,128]{2,0,1:T(8,128)} %all-to-all-done.2, s32[128]{0:T(128)S(1)} %copy-done.13), kind=kOutput, calls=%fused_computation.11 | convolution fusion | flops 150996480 | bytes 4588032 | tf_op jit(solution)/shard_map/qj,kjc->kqc/dot_general | solution.py:138
  (211 shorter events, 88.6 us)
Async XLA Ops:
  0.6 8.1 %collective-permute-start = (bf16[64,1536]{1,0:T(8,128)(2,1)}, bf16[64,1536]{1,0:T(8,128)(2,1)S(1)}, u32[]{:S(2)}, u32[]{:S(2)}) collective-permute-start(bf16[64,1536]{1,0:T(8,128)(2,1)} %param.21), channel_id=1, source_target_pairs={{0,2},{2,4},{4,6},{6,8},{8,10},{10,12},{12,14},{14,16},{16,18},{18... | collective-permute-start | bytes 589832 | tf_op jit(solution)/shard_map/ppermute | solution.py:92
  2.2 20.6 %collective-permute-start.8 = (bf16[64,1536]{1,0:T(8,128)(2,1)}, bf16[64,1536]{1,0:T(8,128)(2,1)S(1)}, u32[]{:S(2)}, u32[]{:S(2)}) collective-permute-start(bf16[64,1536]{1,0:T(8,128)(2,1)} %param.21), channel_id=1, source_target_pairs={{0,30},{2,0},{4,2},{6,4},{8,6},{10,8},{12,10},{14,12},{16,14},{18,... | collective-permute-start | bytes 589832 | tf_op jit(solution)/shard_map/ppermute | solution.py:94
  8.7 10.8 %collective-permute-start.1 = (bf16[64,1536]{1,0:T(8,128)(2,1)S(1)}, bf16[64,1536]{1,0:T(8,128)(2,1)S(1)}, u32[]{:S(2)}, u32[]{:S(2)}) collective-permute-start(bf16[64,1536]{1,0:T(8,128)(2,1)S(1)} %collective-permute-done), channel_id=1, source_target_pairs={{0,2},{2,4},{4,6},{6,8},{8,10},{10,12},{12,14},{14,16},{16,18},{18... | collective-permute-start | bytes 589832 | tf_op jit(solution)/shard_map/ppermute | solution.py:92
  14.0 99.6 %all-to-all-start.1 = ((s32[16,8,1]{1,2,0:T(1,128)}), s32[16,8,1]{1,2,0:T(1,128)S(1)}, u32[]{:S(2)}, u32[]{:S(2)}) async-start(s32[16,8,1]{1,2,0:T(1,128)} %bitcast.12), calls=%async_computation.1 | async-start | bytes 16384 | tf_op jit(solution)/shard_map/all_to_all | solution.py:62
  19.5 7.6 %collective-permute-start.2 = (bf16[64,1536]{1,0:T(8,128)(2,1)S(1)}, bf16[64,1536]{1,0:T(8,128)(2,1)S(1)}, u32[]{:S(2)}, u32[]{:S(2)}) collective-permute-start(bf16[64,1536]{1,0:T(8,128)(2,1)S(1)} %collective-permute-done.1), channel_id=1, source_target_pairs={{0,2},{2,4},{4,6},{6,8},{8,10},{10,12},{12,14},{14,16},{16,18},{18... | collective-permute-start | bytes 589832 | tf_op jit(solution)/shard_map/ppermute | solution.py:92
  22.8 9.3 %collective-permute-start.9 = (bf16[64,1536]{1,0:T(8,128)(2,1)S(1)}, bf16[64,1536]{1,0:T(8,128)(2,1)S(1)}, u32[]{:S(2)}, u32[]{:S(2)}) collective-permute-start(bf16[64,1536]{1,0:T(8,128)(2,1)S(1)} %collective-permute-done.8), channel_id=1, source_target_pairs={{0,30},{2,0},{4,2},{6,4},{8,6},{10,8},{12,10},{14,12},{16,14},{18,... | collective-permute-start | bytes 589832 | tf_op jit(solution)/shard_map/ppermute | solution.py:94
  27.1 7.7 %collective-permute-start.3 = (bf16[64,1536]{1,0:T(8,128)(2,1)S(1)}, bf16[64,1536]{1,0:T(8,128)(2,1)S(1)}, u32[]{:S(2)}, u32[]{:S(2)}) collective-permute-start(bf16[64,1536]{1,0:T(8,128)(2,1)S(1)} %collective-permute-done.2), channel_id=1, source_target_pairs={{0,2},{2,4},{4,6},{6,8},{8,10},{10,12},{12,14},{14,16},{16,18},{18... | collective-permute-start | bytes 589832 | tf_op jit(solution)/shard_map/ppermute | solution.py:92
  32.1 9.4 %collective-permute-start.10 = (bf16[64,1536]{1,0:T(8,128)(2,1)S(1)}, bf16[64,1536]{1,0:T(8,128)(2,1)S(1)}, u32[]{:S(2)}, u32[]{:S(2)}) collective-permute-start(bf16[64,1536]{1,0:T(8,128)(2,1)S(1)} %collective-permute-done.9), channel_id=1, source_target_pairs={{0,30},{2,0},{4,2},{6,4},{8,6},{10,8},{12,10},{14,12},{16,14},{18,... | collective-permute-start | bytes 589832 | tf_op jit(solution)/shard_map/ppermute | solution.py:94
  34.9 9.1 %collective-permute-start.4 = (bf16[64,1536]{1,0:T(8,128)(2,1)S(1)}, bf16[64,1536]{1,0:T(8,128)(2,1)S(1)}, u32[]{:S(2)}, u32[]{:S(2)}) collective-permute-start(bf16[64,1536]{1,0:T(8,128)(2,1)S(1)} %collective-permute-done.3), channel_id=1, source_target_pairs={{0,2},{2,4},{4,6},{6,8},{8,10},{10,12},{12,14},{14,16},{16,18},{18... | collective-permute-start | bytes 589832 | tf_op jit(solution)/shard_map/ppermute | solution.py:92
  41.5 10.3 %collective-permute-start.11 = (bf16[64,1536]{1,0:T(8,128)(2,1)S(1)}, bf16[64,1536]{1,0:T(8,128)(2,1)S(1)}, u32[]{:S(2)}, u32[]{:S(2)}) collective-permute-start(bf16[64,1536]{1,0:T(8,128)(2,1)S(1)} %collective-permute-done.10), channel_id=1, source_target_pairs={{0,30},{2,0},{4,2},{6,4},{8,6},{10,8},{12,10},{14,12},{16,14},{18,... | collective-permute-start | bytes 589832 | tf_op jit(solution)/shard_map/ppermute | solution.py:94
  44.0 10.4 %collective-permute-start.5 = (bf16[64,1536]{1,0:T(8,128)(2,1)S(1)}, bf16[64,1536]{1,0:T(8,128)(2,1)S(1)}, u32[]{:S(2)}, u32[]{:S(2)}) collective-permute-start(bf16[64,1536]{1,0:T(8,128)(2,1)S(1)} %collective-permute-done.4), channel_id=1, source_target_pairs={{0,2},{2,4},{4,6},{6,8},{8,10},{10,12},{12,14},{14,16},{16,18},{18... | collective-permute-start | bytes 589832 | tf_op jit(solution)/shard_map/ppermute | solution.py:92
  51.7 11.8 %collective-permute-start.12 = (bf16[64,1536]{1,0:T(8,128)(2,1)S(1)}, bf16[64,1536]{1,0:T(8,128)(2,1)S(1)}, u32[]{:S(2)}, u32[]{:S(2)}) collective-permute-start(bf16[64,1536]{1,0:T(8,128)(2,1)S(1)} %collective-permute-done.11), channel_id=1, source_target_pairs={{0,30},{2,0},{4,2},{6,4},{8,6},{10,8},{12,10},{14,12},{16,14},{18,... | collective-permute-start | bytes 589832 | tf_op jit(solution)/shard_map/ppermute | solution.py:94
  54.4 11.6 %collective-permute-start.6 = (bf16[64,1536]{1,0:T(8,128)(2,1)S(1)}, bf16[64,1536]{1,0:T(8,128)(2,1)S(1)}, u32[]{:S(2)}, u32[]{:S(2)}) collective-permute-start(bf16[64,1536]{1,0:T(8,128)(2,1)S(1)} %collective-permute-done.5), channel_id=1, source_target_pairs={{0,2},{2,4},{4,6},{6,8},{8,10},{10,12},{12,14},{14,16},{16,18},{18... | collective-permute-start | bytes 589832 | tf_op jit(solution)/shard_map/ppermute | solution.py:92
  63.5 9.2 %collective-permute-start.13 = (bf16[64,1536]{1,0:T(8,128)(2,1)S(1)}, bf16[64,1536]{1,0:T(8,128)(2,1)S(1)}, u32[]{:S(2)}, u32[]{:S(2)}) collective-permute-start(bf16[64,1536]{1,0:T(8,128)(2,1)S(1)} %collective-permute-done.12), channel_id=1, source_target_pairs={{0,30},{2,0},{4,2},{6,4},{8,6},{10,8},{12,10},{14,12},{16,14},{18,... | collective-permute-start | bytes 589832 | tf_op jit(solution)/shard_map/ppermute | solution.py:94
  66.0 9.1 %collective-permute-start.7 = (bf16[64,1536]{1,0:T(8,128)(2,1)S(1)}, bf16[64,1536]{1,0:T(8,128)(2,1)S(1)}, u32[]{:S(2)}, u32[]{:S(2)}) collective-permute-start(bf16[64,1536]{1,0:T(8,128)(2,1)S(1)} %collective-permute-done.6), channel_id=1, source_target_pairs={{0,2},{2,4},{4,6},{6,8},{8,10},{10,12},{12,14},{14,16},{16,18},{18... | collective-permute-start | bytes 589832 | tf_op jit(solution)/shard_map/ppermute | solution.py:92
  72.7 7.5 %collective-permute-start.14 = (bf16[64,1536]{1,0:T(8,128)(2,1)S(1)}, bf16[64,1536]{1,0:T(8,128)(2,1)S(1)}, u32[]{:S(2)}, u32[]{:S(2)}) collective-permute-start(bf16[64,1536]{1,0:T(8,128)(2,1)S(1)} %collective-permute-done.13), channel_id=1, source_target_pairs={{0,30},{2,0},{4,2},{6,4},{8,6},{10,8},{12,10},{14,12},{16,14},{18,... | collective-permute-start | bytes 589832 | tf_op jit(solution)/shard_map/ppermute | solution.py:94
  113.7 108.6 %all-to-all-start = ((f32[64,128,128]{2,0,1:T(8,128)}), f32[64,128,128]{2,0,1:T(8,128)}, u32[]{:S(2)}, u32[]{:S(2)}) async-start(f32[64,128,128]{2,0,1:T(8,128)} %copy.32), calls=%async_computation | async-start | bytes 8388608 | tf_op jit(solution)/shard_map/all_to_all | solution.py:137
  234.4 7.8 %collective-permute-start.16 = (bf16[64,1536]{1,0:T(8,128)(2,1)S(1)}, bf16[64,1536]{1,0:T(8,128)(2,1)S(1)}, u32[]{:S(2)}, u32[]{:S(2)}) collective-permute-start(bf16[64,1536]{1,0:T(8,128)(2,1)S(1)} %collective-permute-done.15), channel_id=1, source_target_pairs={{0,2},{2,4},{4,6},{6,8},{8,10},{10,12},{12,14},{14,16},{16,18},{18... | collective-permute-start | bytes 589832 | tf_op jit(solution)/shard_map/ppermute | solution.py:92
  236.5 8.9 %collective-permute-start.23 = (bf16[64,1536]{1,0:T(8,128)(2,1)S(1)}, bf16[64,1536]{1,0:T(8,128)(2,1)S(1)}, u32[]{:S(2)}, u32[]{:S(2)}) collective-permute-start(bf16[64,1536]{1,0:T(8,128)(2,1)S(1)} %fusion.42), channel_id=1, source_target_pairs={{0,30},{2,0},{4,2},{6,4},{8,6},{10,8},{12,10},{14,12},{16,14},{18,... | collective-permute-start | bytes 589832 | tf_op jit(solution)/shard_map/ppermute | solution.py:94
  242.2 8.4 %collective-permute-start.17 = (bf16[64,1536]{1,0:T(8,128)(2,1)S(1)}, bf16[64,1536]{1,0:T(8,128)(2,1)S(1)}, u32[]{:S(2)}, u32[]{:S(2)}) collective-permute-start(bf16[64,1536]{1,0:T(8,128)(2,1)S(1)} %collective-permute-done.16), channel_id=1, source_target_pairs={{0,2},{2,4},{4,6},{6,8},{8,10},{10,12},{12,14},{14,16},{16,18},{18... | collective-permute-start | bytes 589832 | tf_op jit(solution)/shard_map/ppermute | solution.py:92
  245.4 7.6 %collective-permute-start.24 = (bf16[64,1536]{1,0:T(8,128)(2,1)S(1)}, bf16[64,1536]{1,0:T(8,128)(2,1)S(1)}, u32[]{:S(2)}, u32[]{:S(2)}) collective-permute-start(bf16[64,1536]{1,0:T(8,128)(2,1)S(1)} %collective-permute-done.23), channel_id=1, source_target_pairs={{0,30},{2,0},{4,2},{6,4},{8,6},{10,8},{12,10},{14,12},{16,14},{18,... | collective-permute-start | bytes 589832 | tf_op jit(solution)/shard_map/ppermute | solution.py:94
  250.7 8.7 %collective-permute-start.18 = (bf16[64,1536]{1,0:T(8,128)(2,1)S(1)}, bf16[64,1536]{1,0:T(8,128)(2,1)S(1)}, u32[]{:S(2)}, u32[]{:S(2)}) collective-permute-start(bf16[64,1536]{1,0:T(8,128)(2,1)S(1)} %collective-permute-done.17), channel_id=1, source_target_pairs={{0,2},{2,4},{4,6},{6,8},{8,10},{10,12},{12,14},{14,16},{16,18},{18... | collective-permute-start | bytes 589832 | tf_op jit(solution)/shard_map/ppermute | solution.py:92
  253.0 7.6 %collective-permute-start.25 = (bf16[64,1536]{1,0:T(8,128)(2,1)S(1)}, bf16[64,1536]{1,0:T(8,128)(2,1)S(1)}, u32[]{:S(2)}, u32[]{:S(2)}) collective-permute-start(bf16[64,1536]{1,0:T(8,128)(2,1)S(1)} %collective-permute-done.24), channel_id=1, source_target_pairs={{0,30},{2,0},{4,2},{6,4},{8,6},{10,8},{12,10},{14,12},{16,14},{18,... | collective-permute-start | bytes 589832 | tf_op jit(solution)/shard_map/ppermute | solution.py:94
  259.4 8.0 %collective-permute-start.19 = (bf16[64,1536]{1,0:T(8,128)(2,1)S(1)}, bf16[64,1536]{1,0:T(8,128)(2,1)S(1)}, u32[]{:S(2)}, u32[]{:S(2)}) collective-permute-start(bf16[64,1536]{1,0:T(8,128)(2,1)S(1)} %collective-permute-done.18), channel_id=1, source_target_pairs={{0,2},{2,4},{4,6},{6,8},{8,10},{10,12},{12,14},{14,16},{16,18},{18... | collective-permute-start | bytes 589832 | tf_op jit(solution)/shard_map/ppermute | solution.py:92
  260.5 8.0 %collective-permute-start.26 = (bf16[64,1536]{1,0:T(8,128)(2,1)S(1)}, bf16[64,1536]{1,0:T(8,128)(2,1)S(1)}, u32[]{:S(2)}, u32[]{:S(2)}) collective-permute-start(bf16[64,1536]{1,0:T(8,128)(2,1)S(1)} %collective-permute-done.25), channel_id=1, source_target_pairs={{0,30},{2,0},{4,2},{6,4},{8,6},{10,8},{12,10},{14,12},{16,14},{18,... | collective-permute-start | bytes 589832 | tf_op jit(solution)/shard_map/ppermute | solution.py:94
  267.4 8.7 %collective-permute-start.20 = (bf16[64,1536]{1,0:T(8,128)(2,1)S(1)}, bf16[64,1536]{1,0:T(8,128)(2,1)S(1)}, u32[]{:S(2)}, u32[]{:S(2)}) collective-permute-start(bf16[64,1536]{1,0:T(8,128)(2,1)S(1)} %collective-permute-done.19), channel_id=1, source_target_pairs={{0,2},{2,4},{4,6},{6,8},{8,10},{10,12},{12,14},{14,16},{16,18},{18... | collective-permute-start | bytes 589832 | tf_op jit(solution)/shard_map/ppermute | solution.py:92
  268.6 11.7 %collective-permute-start.27 = (bf16[64,1536]{1,0:T(8,128)(2,1)S(1)}, bf16[64,1536]{1,0:T(8,128)(2,1)S(1)}, u32[]{:S(2)}, u32[]{:S(2)}) collective-permute-start(bf16[64,1536]{1,0:T(8,128)(2,1)S(1)} %collective-permute-done.26), channel_id=1, source_target_pairs={{0,30},{2,0},{4,2},{6,4},{8,6},{10,8},{12,10},{14,12},{16,14},{18,... | collective-permute-start | bytes 589832 | tf_op jit(solution)/shard_map/ppermute | solution.py:94
  276.0 9.7 %collective-permute-start.21 = (bf16[64,1536]{1,0:T(8,128)(2,1)S(1)}, bf16[64,1536]{1,0:T(8,128)(2,1)}, u32[]{:S(2)}, u32[]{:S(2)}) collective-permute-start(bf16[64,1536]{1,0:T(8,128)(2,1)S(1)} %collective-permute-done.20), channel_id=1, source_target_pairs={{0,2},{2,4},{4,6},{6,8},{8,10},{10,12},{12,14},{14,16},{16,18},{18... | collective-permute-start | bytes 589832 | tf_op jit(solution)/shard_map/ppermute | solution.py:92
  280.2 9.5 %collective-permute-start.28 = (bf16[64,1536]{1,0:T(8,128)(2,1)S(1)}, bf16[64,1536]{1,0:T(8,128)(2,1)S(1)}, u32[]{:S(2)}, u32[]{:S(2)}) collective-permute-start(bf16[64,1536]{1,0:T(8,128)(2,1)S(1)} %collective-permute-done.27), channel_id=1, source_target_pairs={{0,30},{2,0},{4,2},{6,4},{8,6},{10,8},{12,10},{14,12},{16,14},{18,... | collective-permute-start | bytes 589832 | tf_op jit(solution)/shard_map/ppermute | solution.py:94
  285.8 6.7 %collective-permute-start.22 = (bf16[64,1536]{1,0:T(8,128)(2,1)}, bf16[64,1536]{1,0:T(8,128)(2,1)S(1)}, u32[]{:S(2)}, u32[]{:S(2)}) collective-permute-start(bf16[64,1536]{1,0:T(8,128)(2,1)} %collective-permute-done.21), channel_id=1, source_target_pairs={{0,2},{2,4},{4,6},{6,8},{8,10},{10,12},{12,14},{14,16},{16,18},{18... | collective-permute-start | bytes 589832 | tf_op jit(solution)/shard_map/ppermute | solution.py:92
  289.8 7.8 %collective-permute-start.29 = (bf16[64,1536]{1,0:T(8,128)(2,1)S(1)}, bf16[64,1536]{1,0:T(8,128)(2,1)S(1)}, u32[]{:S(2)}, u32[]{:S(2)}) collective-permute-start(bf16[64,1536]{1,0:T(8,128)(2,1)S(1)} %collective-permute-done.28), channel_id=1, source_target_pairs={{0,30},{2,0},{4,2},{6,4},{8,6},{10,8},{12,10},{14,12},{16,14},{18,... | collective-permute-start | bytes 589832 | tf_op jit(solution)/shard_map/ppermute | solution.py:94
  331.4 109.7 %all-to-all-start.2 = ((f32[64,128,128]{2,0,1:T(8,128)}), f32[64,128,128]{2,0,1:T(8,128)}, u32[]{:S(2)}, u32[]{:S(2)}) async-start(f32[64,128,128]{2,0,1:T(8,128)} %copy.37), calls=%async_computation.2 | async-start | bytes 8388608 | tf_op jit(solution)/shard_map/all_to_all | solution.py:137
  (43 other events, 1489.0 us)
